TPU v7x, 128 devices: a whole 4x4x4 slice. The times are simulated.
128 devices in a mesh: expert: 16 (over z, x), tensor: 8 (over y, core).
Axes of the slice: x: 4, y: 4, z: 4, core: 2. Of those that a mesh axis runs over, the one named last changes fastest.
Arguments:
- tokens: bfloat16 [2048, 4096], P('expert'), may hold values from -6 to 6
- cotangent: bfloat16 [2048, 4096], P('expert'), may hold values from -6 to 6
- expert_ids: int32 [2048, 8], P('expert'), may hold values from 0 to 127, all different within a row; in each aligned block of 128 rows (0 to 127, 128 to 255, ...) at most 9 rows name the same one
- gate_probs: float32 [2048, 8], P('expert'), may hold values from 0.05 to 1
- w_gate: bfloat16 [128, 896, 4096], P('expert', 'tensor'), may hold values from -0.09375 to 0.09375
- w_up: bfloat16 [128, 896, 4096], P('expert', 'tensor'), may hold values from -0.09375 to 0.09375
- w_down: bfloat16 [128, 896, 4096], P('expert', 'tensor'), may hold values from -0.1875 to 0.1875
Outputs:
- mixed: bfloat16 [2048, 4096], P('expert')
- grad_tokens: bfloat16 [2048, 4096], P('expert')
Inputs may be any that keep to these rules, and one draw needn't show every extreme that they name: `expert_ids`: each token names 8 different experts; the 128 tokens of one index of the expert axis name one expert at most 9 times, a bound that some block reaches.
All inputs are finite; a program needn't handle non-finite values.
Results may differ from a plain program's by a relative error of at most 0.017.
Values may be sent and summed in bfloat16 or wider, within the bound.
A program may use at most 192 MiB of HBM per device.

v0:
```python
import jax
import jax.numpy as jnp
from jax import lax
from jax.sharding import PartitionSpec as P


def expert_work(segment, w_gate, w_up, w_down, features):
    token_part = segment[..., :features]
    scaled_part = segment[..., features:]
    pre_gate = jnp.einsum("sicd,ihd->sich", token_part, w_gate, preferred_element_type=jnp.float32)
    up_value = jnp.einsum("sicd,ihd->sich", token_part, w_up, preferred_element_type=jnp.float32)
    sigmoid_gate = jax.nn.sigmoid(pre_gate)
    activated = pre_gate * sigmoid_gate
    hidden = (activated * up_value).astype(jnp.bfloat16)
    output_rows = jnp.einsum("sich,ihd->sicd", hidden, w_down, preferred_element_type=jnp.float32)
    grad_hidden = jnp.einsum(
        "sicd,ihd->sich", scaled_part, w_down, preferred_element_type=jnp.float32
    )
    grad_gate = (
        grad_hidden * up_value * sigmoid_gate * (1.0 + pre_gate * (1.0 - sigmoid_gate))
    ).astype(jnp.bfloat16)
    grad_up = (grad_hidden * activated).astype(jnp.bfloat16)
    grad_rows = jnp.einsum("sich,ihd->sicd", grad_gate, w_gate, preferred_element_type=jnp.float32)
    grad_rows = grad_rows + jnp.einsum(
        "sich,ihd->sicd", grad_up, w_up, preferred_element_type=jnp.float32
    )
    return jnp.concatenate([output_rows, grad_rows], axis=-1)


def body(tokens, cotangent, expert_ids, gate_probs, w_gate, w_up, w_down):
    tok_count, features = tokens.shape
    top_count = expert_ids.shape[1]
    expert_devs = lax.axis_size("expert")
    tensor_devs = lax.axis_size("tensor")
    local_experts = w_gate.shape[0]
    all_experts = local_experts * expert_devs
    capacity = max(2, 9 * tok_count * top_count // (8 * all_experts))
    own_share = local_experts // tensor_devs
    highest = lax.Precision.HIGHEST
    matches = expert_ids[:, :, None] == jnp.arange(all_experts, dtype=jnp.int32)[None, None, :]
    chosen = jnp.sum(matches.astype(jnp.float32), axis=1)
    prob_table = jnp.sum(jnp.where(matches, gate_probs[:, :, None], 0.0), axis=1)
    positions = jnp.arange(tok_count, dtype=jnp.int32)
    earlier = (positions[:, None] > positions[None, :]).astype(jnp.float32)
    slot_table = jnp.dot(earlier, chosen, precision=highest)
    slot_ids = jnp.arange(capacity, dtype=jnp.float32)
    place = jnp.where(
        chosen.T[:, None, :] > 0.5,
        (slot_table.T[:, None, :] == slot_ids[None, :, None]).astype(jnp.float32),
        0.0,
    )
    token_rows = jnp.einsum(
        "est,td->esd", place.astype(jnp.bfloat16), tokens, preferred_element_type=jnp.float32
    ).astype(jnp.bfloat16)
    place_prob = place * prob_table.T[:, None, :]
    scaled_rows = jnp.einsum(
        "est,td->esd", place_prob, cotangent.astype(jnp.float32), precision=highest
    ).astype(jnp.bfloat16)
    buffer = jnp.concatenate([token_rows, scaled_rows], axis=-1)
    buffer = buffer.reshape(expert_devs, local_experts, capacity, 2 * features)
    arrived = lax.all_to_all(buffer, "expert", split_axis=0, concat_axis=0, tiled=True)
    results = expert_work(arrived, w_gate, w_up, w_down, features)
    reduced = lax.psum_scatter(
        results.astype(jnp.bfloat16), "tensor", scatter_dimension=1, tiled=True
    )
    returned_rows = lax.all_to_all(reduced, "expert", split_axis=0, concat_axis=0, tiled=True)
    row_total = expert_devs * own_share * capacity
    returned_rows = returned_rows.reshape(row_total, 2 * features)
    tensor_place = lax.axis_index("tensor")
    chosen_mine = lax.dynamic_slice_in_dim(
        chosen.reshape(tok_count, expert_devs, tensor_devs, own_share), tensor_place, 1, 2
    )[:, :, 0, :]
    slot_mine = lax.dynamic_slice_in_dim(
        slot_table.reshape(tok_count, expert_devs, tensor_devs, own_share), tensor_place, 1, 2
    )[:, :, 0, :]
    prob_mine = lax.dynamic_slice_in_dim(
        prob_table.reshape(tok_count, expert_devs, tensor_devs, own_share), tensor_place, 1, 2
    )[:, :, 0, :]
    collect = jnp.where(
        chosen_mine[..., None] > 0.5,
        (slot_mine[..., None] == slot_ids[None, None, None, :]).astype(jnp.float32),
        0.0,
    )
    collect_prob = (collect * prob_mine[..., None]).reshape(tok_count, row_total)
    collect = collect.reshape(tok_count, row_total)
    output_part = jnp.dot(
        collect_prob, returned_rows[:, :features].astype(jnp.float32), precision=highest
    )
    input_part = jnp.dot(
        collect.astype(jnp.bfloat16),
        returned_rows[:, features:],
        preferred_element_type=jnp.float32,
    )
    mixed, grad_tokens = (
        lax.psum(output_part.astype(jnp.bfloat16), "tensor").astype(jnp.float32),
        lax.psum(input_part.astype(jnp.bfloat16), "tensor").astype(jnp.float32),
    )
    return (mixed.astype(jnp.bfloat16), grad_tokens.astype(jnp.bfloat16))


def solution(mesh):
    return jax.shard_map(
        body,
        mesh=mesh,
        in_specs=(
            P("expert", None),
            P("expert", None),
            P("expert", None),
            P("expert", None),
            P("expert", "tensor", None),
            P("expert", "tensor", None),
            P("expert", "tensor", None),
        ),
        out_specs=(P("expert", None), P("expert", None)),
        check_vma=False,
    )
```

profile of v0, /device:TPU:0, one launch (start us, length us, event | category | flops | bytes accessed | tf_op | source)
XLA Modules:
  0.0 605.1 jit_solution(26834078855225393)
XLA Ops:
  7.2 0.9 copy.37
  9.8 2.8 convolution_convert_fusion.1
  12.6 9.5 %convolution_convert_fusion = bf16[128,9,4096]{2,0,1:T(8,128)(2,1)} fusion(bf16[128,4096]{1,0:T(8,128)(2,1)S(1)} %copy-done.2, f32[128,128]{1,0:T(8,128)S(1)} %copy.43, f32[128,128]{1,0:T(8,128)S(1)} %bitcast.69, pred[128,128]{1,0:T(8,128)(4,1)S(1)} %copy.42), kind=kOutput, calls=%fused_computation.11 | convolution fusion | flops 7253065728 | bytes 10633216 | tf_op jit(solution)/shard_map/est,td->esd/dot_general | solution.py:56
  22.2 7.2 %maximum_bitcast_fusion = bf16[16,8,9,8192]{3,1,0,2:T(8,128)(2,1)S(1)} fusion(bf16[128,9,4096]{2,0,1:T(8,128)(2,1)} %convolution_convert_fusion, bf16[128,9,4096]{2,0,1:T(8,128)(2,1)S(1)} %convolution_convert_fusion.1), kind=kLoop, calls=%fused_computation | loop fusion | flops 37748736 | bytes 37748736 | tf_op jit(solution)/shard_map/reshape | solution.py:60
  29.4 6.6 %copy.44 = bf16[16,8,9,8192]{3,1,2,0:T(8,128)(2,1)} copy(bf16[16,8,9,8192]{3,1,0,2:T(8,128)(2,1)S(1)} %maximum_bitcast_fusion) | data formatting | bytes 37748736 | tf_op jit(solution)/shard_map/reshape | solution.py:60
  36.0 216.1 %all_to_all.10 = bf16[16,8,9,8192]{3,1,2,0:T(8,128)(2,1)S(1)} all-to-all(bf16[16,8,9,8192]{3,1,2,0:T(8,128)(2,1)} %copy.44), channel_id=1, replica_groups=mesh['expert'=16,'tensor'=8] {'expert'}, dimensions={0} | all-to-all | bytes 37748736 | tf_op jit(solution)/shard_map/all_to_all | solution.py:61
  252.1 7.1 %fusion.60 = (bf16[16,8,9,4096]{3,1,2,0:T(8,128)(2,1)}, bf16[16,8,9,4096]{3,1,2,0:T(8,128)(2,1)}) fusion(bf16[16,8,9,8192]{3,1,2,0:T(8,128)(2,1)S(1)} %all_to_all.10), kind=kLoop, calls=%fused_computation.69 | loop fusion | bytes 37748736 | tf_op jit(solution)/shard_map/slice | solution.py:9
  259.2 11.8 %fusion.14 = f32[16,8,9,112]{3,0,2,1:T(8,128)S(1)} fusion(bf16[8,112,4096]{2,1,0:T(8,128)(2,1)} %param.11, bf16[16,8,9,4096]{3,1,2,0:T(8,128)(2,1)} %get-tuple-element.7), kind=kOutput, calls=%fused_computation.22 | convolution fusion | flops 1056964608 | bytes 17293312 | tf_op jit(solution)/shard_map/sicd,ihd->sich/dot_general | solution.py:10
  271.0 11.9 %fusion.19 = f32[16,8,9,112]{3,0,2,1:T(8,128)S(1)} fusion(bf16[8,112,4096]{2,1,0:T(8,128)(2,1)} %param.12, bf16[16,8,9,4096]{3,1,2,0:T(8,128)(2,1)} %get-tuple-element.7), kind=kOutput, calls=%fused_computation.23 | convolution fusion | flops 1056964608 | bytes 17293312 | tf_op jit(solution)/shard_map/sicd,ihd->sich/dot_general | solution.py:11
  282.9 11.7 %fusion.24 = f32[16,8,9,112]{3,0,2,1:T(8,128)S(1)} fusion(bf16[8,112,4096]{2,1,0:T(8,128)(2,1)} %param.13, bf16[16,8,9,4096]{3,1,2,0:T(8,128)(2,1)} %get-tuple-element.6), kind=kOutput, calls=%fused_computation.24 | convolution fusion | flops 1056964608 | bytes 17293312 | tf_op jit(solution)/shard_map/sicd,ihd->sich/dot_general | solution.py:16
  294.6 9.4 %convert_bitcast_fusion = bf16[16,8,9,4096]{3,0,2,1:T(8,128)(2,1)} fusion(bf16[8,112,4096]{2,1,0:T(8,128)(2,1)} %param.13, f32[16,8,9,112]{3,0,2,1:T(8,128)S(1)} %fusion.19, f32[16,8,9,112]{3,0,2,1:T(8,128)S(1)} %fusion.14), kind=kOutput, calls=%fused_computation.6 | convolution fusion | flops 1062457344 | bytes 17809408 | tf_op jit(solution)/shard_map/sich,ihd->sicd/dot_general | solution.py:15
  304.0 12.2 %fusion.9 = f32[8,16,9,4096]{3,1,2,0:T(8,128)} fusion(bf16[8,112,4096]{2,1,0:T(8,128)(2,1)} %param.11, f32[16,8,9,112]{3,0,2,1:T(8,128)S(1)} %fusion.14, f32[16,8,9,112]{3,0,2,1:T(8,128)S(1)} %fusion.24, f32[16,8,9,112]{3,0,2,1:T(8,128)S(1)} %fusion.19), kind=kOutput, calls=%fused_computation.15 | convolution fusion | flops 1058254848 | bytes 27762688 | tf_op jit(solution)/shard_map/sich,ihd->sicd/dot_general | solution.py:23
  316.2 15.0 %fusion = bf16[16,8,9,4096]{3,0,2,1:T(8,128)(2,1)} fusion(f32[8,16,9,4096]{3,1,2,0:T(8,128)} %fusion.9, bf16[8,112,4096]{2,1,0:T(8,128)(2,1)} %param.12, f32[16,8,9,112]{3,0,2,1:T(8,128)S(1)} %fusion.24, f32[16,8,9,112]{3,0,2,1:T(8,128)S(1)} %fusion.14), kind=kOutput, calls=%fused_computation.3 | convolution fusion | flops 1067175936 | bytes 36683776 | tf_op jit(solution)/shard_map/sich,ihd->sicd/dot_general | solution.py:24
  331.2 16.5 %pad_maximum_fusion = bf16[16,8,9,8192]{3,0,2,1:T(8,128)(2,1)} fusion(bf16[16,8,9,4096]{3,0,2,1:T(8,128)(2,1)} %fusion, bf16[16,8,9,4096]{3,0,2,1:T(8,128)(2,1)} %convert_bitcast_fusion), kind=kLoop, calls=%fused_computation.1 | loop fusion | flops 37748736 | bytes 37748736 | tf_op jit(solution)/shard_map/concatenate | solution.py:27
  347.7 99.5 %reduce-scatter.2.cloned.1.call-done = bf16[16,1,9,8192]{3,0,2,1:T(8,128)(2,1)} async-done(((bf16[16,8,9,8192]{3,0,2,1:T(8,128)(2,1)}), bf16[16,1,9,8192]{3,0,2,1:T(8,128)(2,1)}) %reduce-scatter.2.cloned.1.call-update) | async-done | bytes 2359312 | tf_op jit(solution)/shard_map/reduce_scatter | solution.py:63
  447.1 5.2 copy.47
  452.3 7.0 %all-to-all-start.1 = ((bf16[16,1,9,8192]{3,2,1,0:T(8,128)(2,1)}), bf16[16,1,9,8192]{3,2,1,0:T(8,128)(2,1)}, u32[]{:S(2)}, u32[]{:S(2)}) async-start(bf16[16,1,9,8192]{3,2,1,0:T(8,128)(2,1)} %copy.47), calls=%async_computation.2 | async-start | bytes 8388608 | tf_op jit(solution)/shard_map/all_to_all | solution.py:66
  460.0 60.7 %all-to-all-done.1 = bf16[16,1,9,8192]{3,2,1,0:T(8,128)(2,1)} async-done(((bf16[16,1,9,8192]{3,2,1,0:T(8,128)(2,1)}), bf16[16,1,9,8192]{3,2,1,0:T(8,128)(2,1)}, u32[]{:S(2)}, u32[]{:S(2)}) %all-to-all-start.1) | async-done | bytes 2359328 | tf_op jit(solution)/shard_map/all_to_all | solution.py:66
  520.7 2.8 reshape.49
  523.5 1.5 convolution_convert_fusion.2
  524.9 2.0 convolution_convert_fusion.3
  527.0 66.5 %all-reduce.3.cloned.1.call-done = (bf16[128,4096]{1,0:T(8,128)(2,1)}, bf16[128,4096]{1,0:T(8,128)(2,1)}) async-done(((bf16[128,4096]{1,0:T(8,128)(2,1)}, bf16[128,4096]{1,0:T(8,128)(2,1)}), (bf16[128,4096]{1,0:T(8,128)(2,1)}, bf16[128,4096]{1,0:T(8,128)(2,1)})) %all-reduce.3.cloned.1.call-update) | async-done | bytes 2097168 | tf_op jit(solution)/shard_map/psum | solution.py:95
  593.5 2.3 copy.71
  595.8 2.3 copy.72
  (30 shorter events, 2.2 us)
Async XLA Ops:
  7.2 2.7 copy-start
  7.2 5.4 copy-start.2
  7.2 439.9 %reduce-scatter.2.cloned.1.call-start = ((), (), s32[]{:S(2)}) async-start(), calls=%async_computation.3 | async-start | bytes 21233664 | tf_op jit(solution)/shard_map/reduce_scatter | solution.py:63
  452.3 68.4 %all-to-all-start.1 = ((bf16[16,1,9,8192]{3,2,1,0:T(8,128)(2,1)}), bf16[16,1,9,8192]{3,2,1,0:T(8,128)(2,1)}, u32[]{:S(2)}, u32[]{:S(2)}) async-start(bf16[16,1,9,8192]{3,2,1,0:T(8,128)(2,1)} %copy.47), calls=%async_computation.2 | async-start | bytes 8388608 | tf_op jit(solution)/shard_map/all_to_all | solution.py:66
  459.3 138.8 %copy-start.1 = (bf16[128,4096]{1,0:T(8,128)(2,1)S(1)}, bf16[128,4096]{1,0:T(8,128)(2,1)}, u32[]{:S(2)}) copy-start(bf16[128,4096]{1,0:T(8,128)(2,1)} %param.7) | copy-start | bytes 3145732
  459.3 134.2 %all-reduce.3.cloned.1.call-start = ((), (), s32[]{:S(2)}) async-start(), calls=%async_computation.4 | async-start | bytes 4194304 | tf_op jit(solution)/shard_map/psum | solution.py:95
Sparse Core Ops, SparseCore 0:
  347.8 99.2 reduce-scatter.1
  527.1 66.3 all-reduce.2
where the time goes:
time: 610 us; the launch traced here: 605 us
  waiting for transfers between devices  227 us (37%)
  blocking collectives  216 us (35%)
  matrix products  88 us (14%)
  local copies, waits for them, and re-layouts  28.6 us (5%)
  other arithmetic  24.2 us (4%)
  between operations  14.5 us (2%)
  starting transfers between devices  7.09 us (1%)
    all_to_all x1, blocking collectives, body(): lax.all_to_all(buffer, 'expert', split_axis=0, concat_axis=0, tiled=True)  216 us
    reduce_scatter x1, waiting for transfers between devices, body(): lax.psum_scatter(results.astype(jnp.bfloat16), 'tensor', scatter_dimensio...  99.5 us
    psum x1, waiting for transfers between devices, body(): lax.psum(output_part.astype(jnp.bfloat16), 'tensor').astype(jnp.float32)  66.5 us
    all_to_all x1, waiting for transfers between devices, body(): lax.all_to_all(reduced, 'expert', split_axis=0, concat_axis=0, tiled=True)  60.7 us
    concatenate x1, other arithmetic, expert_work(): return jnp.concatenate([output_rows, grad_rows], axis=-1)  16.5 us
    dot_general x1, matrix products, expert_work(): jnp.einsum('sich,ihd->sicd', grad_up, w_up, preferred_element_type=jnp.fl...  15 us
  transfers between devices with their start and end apart: 3, of which 3 were waited for; matrix products, arithmetic and copies ran while one was open for 0% of the time, Pallas kernels for 0%

commit v1 on v0

--- a/solution.py
+++ b/solution.py
@@ -92,7 +92,9 @@
         preferred_element_type=jnp.float32,
     )
     mixed, grad_tokens = (
-        lax.psum(output_part.astype(jnp.bfloat16), "tensor").astype(jnp.float32),
+        jnp.sum(lax.all_gather(output_part.astype(jnp.bfloat16), "tensor"), axis=0).astype(
+            jnp.float32
+        ),
         lax.psum(input_part.astype(jnp.bfloat16), "tensor").astype(jnp.float32),
     )
     return (mixed.astype(jnp.bfloat16), grad_tokens.astype(jnp.bfloat16))

time: 610 us -> 655 us (1.074)
  waiting for transfers between devices: 227 us -> 268 us
    all_gather x0 -> x1, waiting for transfers between devices: none -> 48.8 us  [body(): lax.all_gather(output_part.astype(jnp.bfloat16), 'tensor')]
    psum x1, waiting for transfers between devices: 66.5 us -> 58.9 us  [body(): lax.psum(input_part.astype(jnp.bfloat16), 'tensor').astype(jnp.float32)]
  transfers between devices with their start and end apart: 3 -> 4, of which waited for: 3 -> 4; matrix products, arithmetic and copies ran while one was open for 0% -> 1% of each run, Pallas kernels for 0% -> 0%
where the time goes in v1:
time: 655 us; the launch traced here: 650 us
  waiting for transfers between devices  268 us (41%)
  blocking collectives  216 us (33%)
  matrix products  87.9 us (13%)
  other arithmetic  30.3 us (5%)
  local copies, waits for them, and re-layouts  26.4 us (4%)
  between operations  14.2 us (2%)
  starting transfers between devices  7.13 us (1%)
    all_to_all x1, blocking collectives, body(): lax.all_to_all(buffer, 'expert', split_axis=0, concat_axis=0, tiled=True)  216 us
    reduce_scatter x1, waiting for transfers between devices, body(): lax.psum_scatter(results.astype(jnp.bfloat16), 'tensor', scatter_dimensio...  99.5 us
    all_to_all x1, waiting for transfers between devices, body(): lax.all_to_all(reduced, 'expert', split_axis=0, concat_axis=0, tiled=True)  60.8 us
    psum x1, waiting for transfers between devices, body(): lax.psum(input_part.astype(jnp.bfloat16), 'tensor').astype(jnp.float32)  58.9 us
    all_gather x1, waiting for transfers between devices, body(): lax.all_gather(output_part.astype(jnp.bfloat16), 'tensor')  48.8 us
    concatenate x1, other arithmetic, expert_work(): return jnp.concatenate([output_rows, grad_rows], axis=-1)  16.5 us
    dot_general x1, matrix products, expert_work(): jnp.einsum('sich,ihd->sicd', grad_up, w_up, preferred_element_type=jnp.fl...  15 us
  transfers between devices with their start and end apart: 4, of which 4 were waited for; matrix products, arithmetic and copies ran while one was open for 1% of the time, Pallas kernels for 0%

profile of v1, /device:TPU:0, one launch (start us, length us, event | category | flops | bytes accessed | tf_op | source)
XLA Modules:
  0.0 650.0 jit_solution(15617524272406490814)
XLA Ops:
  9.8 2.8 convolution_convert_fusion.1
  12.6 9.6 %convolution_convert_fusion = bf16[128,9,4096]{2,0,1:T(8,128)(2,1)} fusion(bf16[128,4096]{1,0:T(8,128)(2,1)S(1)} %copy-done.2, f32[128,128]{1,0:T(8,128)S(1)} %copy.43, f32[128,128]{1,0:T(8,128)S(1)} %bitcast.71, pred[128,128]{1,0:T(8,128)(4,1)S(1)} %copy.42), kind=kOutput, calls=%fused_computation.11 | convolution fusion | flops 7253065728 | bytes 10633216 | tf_op jit(solution)/shard_map/est,td->esd/dot_general | solution.py:56
  22.2 7.2 %maximum_bitcast_fusion = bf16[16,8,9,8192]{3,1,0,2:T(8,128)(2,1)S(1)} fusion(bf16[128,9,4096]{2,0,1:T(8,128)(2,1)} %convolution_convert_fusion, bf16[128,9,4096]{2,0,1:T(8,128)(2,1)S(1)} %convolution_convert_fusion.1), kind=kLoop, calls=%fused_computation | loop fusion | flops 37748736 | bytes 37748736 | tf_op jit(solution)/shard_map/reshape | solution.py:60
  29.4 6.6 %copy.44 = bf16[16,8,9,8192]{3,1,2,0:T(8,128)(2,1)} copy(bf16[16,8,9,8192]{3,1,0,2:T(8,128)(2,1)S(1)} %maximum_bitcast_fusion) | data formatting | bytes 37748736 | tf_op jit(solution)/shard_map/reshape | solution.py:60
  36.0 216.1 %all_to_all.10 = bf16[16,8,9,8192]{3,1,2,0:T(8,128)(2,1)S(1)} all-to-all(bf16[16,8,9,8192]{3,1,2,0:T(8,128)(2,1)} %copy.44), channel_id=1, replica_groups=mesh['expert'=16,'tensor'=8] {'expert'}, dimensions={0} | all-to-all | bytes 37748736 | tf_op jit(solution)/shard_map/all_to_all | solution.py:61
  252.2 7.1 %fusion.60 = (bf16[16,8,9,4096]{3,1,2,0:T(8,128)(2,1)}, bf16[16,8,9,4096]{3,1,2,0:T(8,128)(2,1)}) fusion(bf16[16,8,9,8192]{3,1,2,0:T(8,128)(2,1)S(1)} %all_to_all.10), kind=kLoop, calls=%fused_computation.69 | loop fusion | bytes 37748736 | tf_op jit(solution)/shard_map/slice | solution.py:9
  259.3 11.7 %fusion.14 = f32[16,8,9,112]{3,0,2,1:T(8,128)S(1)} fusion(bf16[8,112,4096]{2,1,0:T(8,128)(2,1)} %param.11, bf16[16,8,9,4096]{3,1,2,0:T(8,128)(2,1)} %get-tuple-element.5), kind=kOutput, calls=%fused_computation.22 | convolution fusion | flops 1056964608 | bytes 17293312 | tf_op jit(solution)/shard_map/sicd,ihd->sich/dot_general | solution.py:10
  271.0 11.9 %fusion.19 = f32[16,8,9,112]{3,0,2,1:T(8,128)S(1)} fusion(bf16[8,112,4096]{2,1,0:T(8,128)(2,1)} %param.12, bf16[16,8,9,4096]{3,1,2,0:T(8,128)(2,1)} %get-tuple-element.5), kind=kOutput, calls=%fused_computation.23 | convolution fusion | flops 1056964608 | bytes 17293312 | tf_op jit(solution)/shard_map/sicd,ihd->sich/dot_general | solution.py:11
  282.9 11.7 %fusion.24 = f32[16,8,9,112]{3,0,2,1:T(8,128)S(1)} fusion(bf16[8,112,4096]{2,1,0:T(8,128)(2,1)} %param.13, bf16[16,8,9,4096]{3,1,2,0:T(8,128)(2,1)} %get-tuple-element.4), kind=kOutput, calls=%fused_computation.24 | convolution fusion | flops 1056964608 | bytes 17293312 | tf_op jit(solution)/shard_map/sicd,ihd->sich/dot_general | solution.py:16
  294.6 9.4 %convert_bitcast_fusion = bf16[16,8,9,4096]{3,0,2,1:T(8,128)(2,1)} fusion(bf16[8,112,4096]{2,1,0:T(8,128)(2,1)} %param.13, f32[16,8,9,112]{3,0,2,1:T(8,128)S(1)} %fusion.19, f32[16,8,9,112]{3,0,2,1:T(8,128)S(1)} %fusion.14), kind=kOutput, calls=%fused_computation.6 | convolution fusion | flops 1062457344 | bytes 17809408 | tf_op jit(solution)/shard_map/sich,ihd->sicd/dot_general | solution.py:15
  304.0 12.2 %fusion.9 = f32[8,16,9,4096]{3,1,2,0:T(8,128)} fusion(bf16[8,112,4096]{2,1,0:T(8,128)(2,1)} %param.11, f32[16,8,9,112]{3,0,2,1:T(8,128)S(1)} %fusion.14, f32[16,8,9,112]{3,0,2,1:T(8,128)S(1)} %fusion.24, f32[16,8,9,112]{3,0,2,1:T(8,128)S(1)} %fusion.19), kind=kOutput, calls=%fused_computation.15 | convolution fusion | flops 1058254848 | bytes 27762688 | tf_op jit(solution)/shard_map/sich,ihd->sicd/dot_general | solution.py:23
  316.2 15.0 %fusion = bf16[16,8,9,4096]{3,0,2,1:T(8,128)(2,1)} fusion(f32[8,16,9,4096]{3,1,2,0:T(8,128)} %fusion.9, bf16[8,112,4096]{2,1,0:T(8,128)(2,1)} %param.12, f32[16,8,9,112]{3,0,2,1:T(8,128)S(1)} %fusion.24, f32[16,8,9,112]{3,0,2,1:T(8,128)S(1)} %fusion.14), kind=kOutput, calls=%fused_computation.3 | convolution fusion | flops 1067175936 | bytes 36683776 | tf_op jit(solution)/shard_map/sich,ihd->sicd/dot_general | solution.py:24
  331.1 16.5 %pad_maximum_fusion = bf16[16,8,9,8192]{3,0,2,1:T(8,128)(2,1)} fusion(bf16[16,8,9,4096]{3,0,2,1:T(8,128)(2,1)} %fusion, bf16[16,8,9,4096]{3,0,2,1:T(8,128)(2,1)} %convert_bitcast_fusion), kind=kLoop, calls=%fused_computation.1 | loop fusion | flops 37748736 | bytes 37748736 | tf_op jit(solution)/shard_map/concatenate | solution.py:27
  347.7 99.5 %reduce-scatter.2.cloned.1.call-done = bf16[16,1,9,8192]{3,0,2,1:T(8,128)(2,1)} async-done(((bf16[16,8,9,8192]{3,0,2,1:T(8,128)(2,1)}), bf16[16,1,9,8192]{3,0,2,1:T(8,128)(2,1)}) %reduce-scatter.2.cloned.1.call-update) | async-done | bytes 2359312 | tf_op jit(solution)/shard_map/reduce_scatter | solution.py:63
  447.2 5.1 copy.47
  452.3 7.0 %all-to-all-start.1 = ((bf16[16,1,9,8192]{3,2,1,0:T(8,128)(2,1)}), bf16[16,1,9,8192]{3,2,1,0:T(8,128)(2,1)}, u32[]{:S(2)}, u32[]{:S(2)}) async-start(bf16[16,1,9,8192]{3,2,1,0:T(8,128)(2,1)} %copy.47), calls=%async_computation.2 | async-start | bytes 8388608 | tf_op jit(solution)/shard_map/all_to_all | solution.py:66
  460.0 60.8 %all-to-all-done.1 = bf16[16,1,9,8192]{3,2,1,0:T(8,128)(2,1)} async-done(((bf16[16,1,9,8192]{3,2,1,0:T(8,128)(2,1)}), bf16[16,1,9,8192]{3,2,1,0:T(8,128)(2,1)}, u32[]{:S(2)}, u32[]{:S(2)}) %all-to-all-start.1) | async-done | bytes 2359328 | tf_op jit(solution)/shard_map/all_to_all | solution.py:66
  520.8 2.9 reshape.49
  523.7 2.0 convolution_convert_fusion.3
  525.8 1.4 convolution_convert_fusion.2
  527.2 48.8 %all-gather.3.cloned.1.call-done = bf16[1024,4096]{1,0:T(8,128)(2,1)} async-done(((bf16[128,4096]{1,0:T(8,128)(2,1)}), bf16[1024,4096]{1,0:T(8,128)(2,1)}) %all-gather.3.cloned.1.call-update) | async-done | bytes 8388624 | tf_op jit(solution)/shard_map/all_gather | solution.py:95
  576.0 6.1 reduce_sum.32
  582.1 58.9 %all-reduce.2.cloned.1.call-done = bf16[128,4096]{1,0:T(8,128)(2,1)} async-done(((bf16[128,4096]{1,0:T(8,128)(2,1)}), bf16[128,4096]{1,0:T(8,128)(2,1)}) %all-reduce.2.cloned.1.call-update) | async-done | bytes 1048592 | tf_op jit(solution)/shard_map/psum | solution.py:98
  641.0 2.3 copy.70
  (33 shorter events, 3.2 us)
Async XLA Ops:
  7.2 2.7 copy-start
  7.2 5.4 copy-start.2
  7.2 440.0 %reduce-scatter.2.cloned.1.call-start = ((), (), s32[]{:S(2)}) async-start(), calls=%async_computation.3 | async-start | bytes 21233664 | tf_op jit(solution)/shard_map/reduce_scatter | solution.py:63
  452.3 68.5 %all-to-all-start.1 = ((bf16[16,1,9,8192]{3,2,1,0:T(8,128)(2,1)}), bf16[16,1,9,8192]{3,2,1,0:T(8,128)(2,1)}, u32[]{:S(2)}, u32[]{:S(2)}) async-start(bf16[16,1,9,8192]{3,2,1,0:T(8,128)(2,1)} %copy.47), calls=%async_computation.2 | async-start | bytes 8388608 | tf_op jit(solution)/shard_map/all_to_all | solution.py:66
  459.3 116.7 %all-gather.3.cloned.1.call-start = ((), (), s32[]{:S(2)}) async-start(), calls=%async_computation.5 | async-start | bytes 9437184 | tf_op jit(solution)/shard_map/all_gather | solution.py:95
  520.8 122.5 %copy-start.1 = (bf16[128,4096]{1,0:T(8,128)(2,1)S(1)}, bf16[128,4096]{1,0:T(8,128)(2,1)}, u32[]{:S(2)}) copy-start(bf16[128,4096]{1,0:T(8,128)(2,1)} %param.7) | copy-start | bytes 3145732
  525.7 115.3 %all-reduce.2.cloned.1.call-start = ((), (), s32[]{:S(2)}) async-start(), calls=%async_computation.4 | async-start | bytes 2097152 | tf_op jit(solution)/shard_map/psum | solution.py:98
Sparse Core Ops, SparseCore 0:
  347.8 99.2 reduce-scatter.1
  525.8 50.1 all-gather.2
  578.4 62.5 all-reduce.1
